TPU v7x, 32 devices: a whole 2x2x4 slice. The times are simulated.
32 devices in a mesh: fsdp: 4 (over x, core), context: 4 (over z), tensor: 2 (over y).
Axes of the slice: x: 2, y: 2, z: 4, core: 2. Of those that a mesh axis runs over, the one named last changes fastest.
Arguments:
- block_input: float32 [8192, 768], P(('fsdp', 'context')), may hold values from -18 to 18
- ln1_gain: float32 [768], replicated, may hold values from 0.1 to 1.9
- ln1_shift: float32 [768], replicated, may hold values from -3 to 3
- qkv_weight: float32 [768, 3, 768], P(('fsdp', 'context'), None, 'tensor'), may hold values from -0.21875 to 0.21875
- qkv_bias: float32 [3, 768], P(None, 'tensor'), may hold values from -3 to 3
- feat_query: float32 [12, 64, 64], P('tensor'), may hold values from -1.5 to 1.5
- feat_key: float32 [12, 64, 64], P('tensor'), may hold values from -1.5 to 1.5
- out_weight: float32 [768, 768], P('tensor', ('fsdp', 'context')), may hold values from -3.5 to 3.5
- out_bias: float32 [768], replicated, may hold values from -3 to 3
- ln2_gain: float32 [768], replicated, may hold values from 0.1 to 1.9
- ln2_shift: float32 [768], replicated, may hold values from -3 to 3
- up_weight: float32 [768, 3072], P(('fsdp', 'context'), 'tensor'), may hold values from -0.21875 to 0.21875
- up_bias: float32 [3072], P('tensor'), may hold values from -3 to 3
- down_weight: float32 [3072, 768], P('tensor', ('fsdp', 'context')), may hold values from -0.109375 to 0.109375
- down_bias: float32 [768], replicated, may hold values from -3 to 3
- lengths: int32 [4], replicated, may hold values from 1024 to 2048, as said below
- deal: int32 [128], P(('fsdp', 'context')), may hold values from 0 to 127, as said below
- cotangent: float32 [8192, 768], P(('fsdp', 'context')), may hold values from -6 to 6
Outputs:
- dealt_output: float32 [128, 64, 768], P(('fsdp', 'context'), 'tensor')
- rms: float32 [3], replicated
- grad_input: float32 [8192, 768], P(('fsdp', 'context'))
- grad_ln1_gain: float32 [768], replicated
- grad_ln1_shift: float32 [768], replicated
- grad_qkv_weight: float32 [768, 3, 768], P(('fsdp', 'context'), None, 'tensor')
- grad_qkv_bias: float32 [3, 768], P(None, 'tensor')
- grad_feat_query: float32 [12, 64, 64], P('tensor')
- grad_feat_key: float32 [12, 64, 64], P('tensor')
- grad_out_weight: float32 [768, 768], P('tensor', ('fsdp', 'context'))
- grad_out_bias: float32 [768], replicated
- grad_ln2_gain: float32 [768], replicated
- grad_ln2_shift: float32 [768], replicated
- grad_up_weight: float32 [768, 3072], P(('fsdp', 'context'), 'tensor')
- grad_up_bias: float32 [3072], P('tensor')
- grad_down_weight: float32 [3072, 768], P('tensor', ('fsdp', 'context'))
- grad_down_bias: float32 [768], replicated
Inputs may be any that keep to these rules, and one draw needn't show every extreme that they name: Sequence lengths; the 4 lengths sum to exactly 8160, and the last of them is exactly 2048. deal is a permutation of the 128 groups. Group j of the device with fsdp index f and context index e (groups numbered along fsdp, then context, then position) goes to position (f * 4 + d) * 8 + e * 2 + r, where the 8 groups of one device take every pair of d < 4 and r < 2 once.
All inputs are finite; a program needn't handle non-finite values.
Results may differ from a plain program's by a relative error of at most 0.0003.
Values sent between devices are 32-bit elements; how exact they have to be, the bound alone decides.
No kernel may reach another device: no remote copies, remote signals or barrier semaphores. Data moves between devices by JAX's collectives and lax.ppermute only.
A program may use at most 128 MiB of HBM per device.

v0:
```python
from functools import partial
import jax
import jax.numpy as jnp
from jax import lax
from jax.sharding import PartitionSpec as P

HIGH = lax.Precision.HIGHEST
NORM_EPS = 1e-05


def entering(x, axis, combine, identity, reverse):
    count, place = (lax.axis_size(axis), lax.axis_index(axis))
    everything = jax.tree.map(lambda part: lax.all_gather(part, axis), x)
    start = jax.tree.map(
        lambda part, zero: jnp.broadcast_to(jnp.asarray(zero, part.dtype), part.shape), x, identity
    )

    def lap(k, before):
        at = count - 1 - k if reverse else k
        reached = at > place if reverse else at < place
        new = combine(before, jax.tree.map(lambda part: part[at], everything))
        return jax.tree.map(lambda a, b: jnp.where(reached, a, b), new, before)

    return lax.fori_loop(0, count, lap, start)


def layer_norm(values, gain, shift):
    middle = jnp.mean(values, axis=-1, keepdims=True)
    centred = values - middle
    spread = jnp.mean(centred * centred, axis=-1, keepdims=True)
    return centred * lax.rsqrt(spread + NORM_EPS) * gain + shift


def feature_map(heads, weight):
    logits = jnp.einsum("rhd,hde->rhe", heads, weight, precision=HIGH)
    return jnp.concatenate(
        [jax.nn.softmax(logits, axis=-1), jax.nn.softmax(-logits, axis=-1)], axis=-1
    )


def segment_of(places, ends, total, number):
    found = jnp.sum((ends[None, :] <= places[:, None]).astype(jnp.int32), axis=1)
    found = jnp.where(places < 0, -1, found)
    return jnp.where(places >= total, number + 1, found)


def project(normed, weight, bias):
    return jnp.einsum("rd,dke->rke", normed, weight, precision=HIGH) + bias


def mlp_part(normed, up_full, up_bias, down_full):
    active = jax.nn.gelu(jnp.dot(normed, up_full, precision=HIGH) + up_bias, approximate=True)
    return jnp.dot(active, down_full, precision=HIGH)


def chain_join(earlier, later):
    passing = 1.0 - later[2]
    return (
        later[0] + passing * earlier[0],
        later[1] + passing * earlier[1],
        jnp.maximum(earlier[2], later[2]),
    )


def local_part(queries, keys, values, weight_q, weight_k, segment, seg_first, block):
    phi_q = feature_map(queries, weight_q)
    phi_k = feature_map(keys, weight_k)
    count_rows, local_heads, head_dim = values.shape
    feats = phi_q.shape[2]
    blocks = count_rows // block
    lower = jnp.arange(block)[:, None] >= jnp.arange(block)[None, :]

    def block_step(carry, pieces):
        state, normer, seg_carry = carry
        piece_q, piece_k, piece_v, seg_piece = pieces
        allowed = jnp.logical_and(lower, seg_piece[:, None] == seg_piece[None, :]).astype(
            jnp.float32
        )
        scores = jnp.einsum("ihf,jhf->hij", piece_q, piece_k, precision=HIGH) * allowed[None]
        numer = jnp.einsum("hij,jhd->ihd", scores, piece_v, precision=HIGH)
        denom = jnp.einsum("hij->ih", scores)
        carried = (seg_piece == seg_carry).astype(jnp.float32)
        numer = numer + carried[:, None, None] * jnp.einsum(
            "ihf,hfd->ihd", piece_q, state, precision=HIGH
        )
        denom = denom + carried[:, None] * jnp.einsum("ihf,hf->ih", piece_q, normer, precision=HIGH)
        final_seg = seg_piece[-1]
        stays = (final_seg == seg_carry).astype(jnp.float32)
        tail_k = piece_k * (seg_piece == final_seg).astype(jnp.float32)[:, None, None]
        state = stays * state + jnp.einsum("jhf,jhd->hfd", tail_k, piece_v, precision=HIGH)
        normer = stays * normer + jnp.sum(tail_k, axis=0)
        return ((state, normer, final_seg), (numer, denom))

    def blocked(array):
        return array.reshape((blocks, block) + array.shape[1:])

    start = (
        jnp.zeros((local_heads, feats, head_dim), jnp.float32),
        jnp.zeros((local_heads, feats), jnp.float32),
        seg_first,
    )
    (state, normer, _), (numer, denom) = lax.scan(
        jax.checkpoint(block_step),
        start,
        (blocked(phi_q), blocked(phi_k), blocked(values), blocked(segment)),
    )
    return (
        phi_q,
        numer.reshape(count_rows, local_heads, head_dim),
        denom.reshape(count_rows, local_heads),
        state,
        normer,
    )


def body(
    block_input,
    ln1_gain,
    ln1_shift,
    qkv_weight,
    qkv_bias,
    feat_query,
    feat_key,
    out_weight,
    out_bias,
    ln2_gain,
    ln2_shift,
    up_weight,
    up_bias,
    down_weight,
    down_bias,
    lengths,
    deal,
    cotangent,
):
    count_rows, width = block_input.shape
    local_heads, head_dim = (feat_query.shape[0], feat_query.shape[1])
    local_width = local_heads * head_dim
    offset = lax.axis_index(("fsdp", "context")) * count_rows
    total = count_rows * lax.axis_size(("fsdp", "context"))
    ends = jnp.cumsum(lengths)
    used = ends[-1]
    number = lengths.shape[0]
    places = offset + jnp.arange(count_rows, dtype=jnp.int32)
    segment = segment_of(places, ends, total, number)
    edges = segment_of(offset + jnp.array([-1, count_rows], dtype=jnp.int32), ends, total, number)
    seg_first = segment[0]
    seg_final = segment[-1]
    carry_in = (edges[0] == seg_first).astype(jnp.float32)
    breaks = (edges[0] != seg_final).astype(jnp.float32)
    valid = (places < used).astype(jnp.float32)[:, None]
    block = min(512, count_rows)
    qkv_full, out_full, up_full, down_full = (
        lax.all_gather(qkv_weight, ("fsdp", "context"), axis=0, tiled=True),
        lax.all_gather(out_weight, ("fsdp", "context"), axis=1, tiled=True),
        lax.all_gather(up_weight, ("fsdp", "context"), axis=0, tiled=True),
        lax.all_gather(down_weight, ("fsdp", "context"), axis=1, tiled=True),
    )
    normed1 = layer_norm(block_input, ln1_gain, ln1_shift)
    qkv = project(normed1, qkv_full, qkv_bias)
    queries = qkv[:, 0, :].reshape(count_rows, local_heads, head_dim)
    keys = qkv[:, 1, :].reshape(count_rows, local_heads, head_dim)
    values = qkv[:, 2, :].reshape(count_rows, local_heads, head_dim)
    attend_local = partial(local_part, segment=segment, seg_first=seg_first, block=block)
    phi_q, numer_local, denom_local, state_tail, norm_tail = attend_local(
        queries, keys, values, feat_query, feat_key
    )
    identity = (jnp.zeros_like(state_tail), jnp.zeros_like(norm_tail), jnp.zeros((), jnp.float32))
    state_scan, norm_scan, _ = entering(
        (state_tail, norm_tail, breaks), ("fsdp", "context"), chain_join, identity, False
    )
    state_in = carry_in * state_scan
    norm_in = carry_in * norm_scan
    first_rows = (segment == seg_first).astype(jnp.float32)[:, None, None]
    masked_q = phi_q * first_rows
    numer = numer_local + jnp.einsum("rhf,hfd->rhd", masked_q, state_in, precision=HIGH)
    denom = denom_local + jnp.einsum("rhf,hf->rh", masked_q, norm_in, precision=HIGH)
    attended = numer / denom[:, :, None]
    attended_flat = attended.reshape(count_rows, local_width)
    attn_part = jnp.dot(attended_flat, out_full, precision=HIGH)
    attn = lax.psum(attn_part, "tensor") + out_bias
    hidden = block_input + attn
    normed2 = layer_norm(hidden, ln2_gain, ln2_shift)
    slots = deal.shape[0]
    group_rows = count_rows // slots
    part_rows = group_rows // lax.axis_size("tensor")
    part_start = lax.axis_index("tensor") * part_rows
    per_peer = slots // lax.axis_size("context")
    slot_of = deal // slots % lax.axis_size("context") * per_peer + deal % per_peer
    counting = jnp.arange(slots, dtype=jnp.int32)
    source_of = jnp.sum(
        jnp.where(slot_of[None, :] == counting[:, None], counting[None, :], 0), axis=1
    )
    mlp_terms = mlp_part(normed2, up_full, up_bias, down_full)
    mlp = lax.psum(mlp_terms, "tensor") + down_bias
    result = hidden + mlp
    outbound = jnp.take(result.reshape(slots, group_rows, width), source_of, axis=0)
    dealt_whole = lax.all_to_all(outbound, "context", split_axis=0, concat_axis=0, tiled=True)
    dealt_output = lax.dynamic_slice_in_dim(dealt_whole, part_start, part_rows, 1)
    squares = jnp.stack(
        [jnp.sum(valid * result * result), jnp.sum(valid * attn * attn), jnp.sum(valid * mlp * mlp)]
    )
    inbound = lax.all_to_all(
        cotangent.reshape(slots, group_rows, width),
        "context",
        split_axis=0,
        concat_axis=0,
        tiled=True,
    )
    grad_y = jnp.take(inbound, slot_of, axis=0).reshape(count_rows, width) * valid
    grad_down_bias = jnp.sum(grad_y, axis=0)
    _, mlp_backward = jax.vjp(mlp_part, normed2, up_full, up_bias, down_full)
    grad_normed2_part, grad_up_full, grad_up_bias, grad_down_full = mlp_backward(grad_y)
    grad_normed2 = lax.psum(grad_normed2_part, "tensor")
    _, norm2_backward = jax.vjp(layer_norm, hidden, ln2_gain, ln2_shift)
    grad_hidden_norm, grad_ln2_gain, grad_ln2_shift = norm2_backward(grad_normed2)
    grad_hidden = grad_y + grad_hidden_norm
    grad_out_bias = jnp.sum(grad_hidden, axis=0)
    grad_out_full = jnp.einsum("rd,re->de", attended_flat, grad_hidden, precision=HIGH)
    grad_attended = jnp.einsum("re,de->rd", grad_hidden, out_full, precision=HIGH).reshape(
        count_rows, local_heads, head_dim
    )
    grad_numer = grad_attended / denom[:, :, None]
    grad_denom = -jnp.sum(grad_attended * attended, axis=2) / denom
    grad_state_in = carry_in * jnp.einsum("rhf,rhd->hfd", masked_q, grad_numer, precision=HIGH)
    grad_norm_in = carry_in * jnp.einsum("rhf,rh->hf", masked_q, grad_denom, precision=HIGH)
    grad_phi_extra = first_rows * (
        jnp.einsum("rhd,hfd->rhf", grad_numer, state_in, precision=HIGH)
        + grad_denom[:, :, None] * norm_in[None, :, :]
    )
    grad_state_tail, grad_norm_tail, _ = entering(
        (grad_state_in, grad_norm_in, breaks), ("fsdp", "context"), chain_join, identity, True
    )
    _, attention_backward = jax.vjp(attend_local, queries, keys, values, feat_query, feat_key)
    grad_queries, grad_keys, grad_values, grad_feat_query, grad_feat_key = attention_backward(
        (grad_phi_extra, grad_numer, grad_denom, grad_state_tail, grad_norm_tail)
    )
    grad_qkv = jnp.stack(
        [
            grad_queries.reshape(count_rows, local_width),
            grad_keys.reshape(count_rows, local_width),
            grad_values.reshape(count_rows, local_width),
        ],
        axis=1,
    )
    _, project_backward = jax.vjp(project, normed1, qkv_full, qkv_bias)
    grad_normed1_part, grad_qkv_full, grad_qkv_bias = project_backward(grad_qkv)
    grad_normed1 = lax.psum(grad_normed1_part, "tensor")
    _, norm1_backward = jax.vjp(layer_norm, block_input, ln1_gain, ln1_shift)
    grad_input_norm, grad_ln1_gain, grad_ln1_shift = norm1_backward(grad_normed1)
    grad_input = grad_hidden + grad_input_norm
    grad_qkv_weight, grad_out_weight, grad_up_weight, grad_down_weight = (
        lax.psum_scatter(grad_qkv_full, ("fsdp", "context"), scatter_dimension=0, tiled=True),
        lax.psum_scatter(grad_out_full, ("fsdp", "context"), scatter_dimension=1, tiled=True),
        lax.psum_scatter(grad_up_full, ("fsdp", "context"), scatter_dimension=0, tiled=True),
        lax.psum_scatter(grad_down_full, ("fsdp", "context"), scatter_dimension=1, tiled=True),
    )
    summed = lax.psum(
        (
            grad_ln1_gain,
            grad_ln1_shift,
            grad_qkv_bias,
            grad_feat_query,
            grad_feat_key,
            grad_out_bias,
            grad_ln2_gain,
            grad_ln2_shift,
            grad_up_bias,
            grad_down_bias,
            squares,
        ),
        ("fsdp", "context"),
    )
    rms = jnp.sqrt(summed[10] / (used.astype(jnp.float32) * width))
    return (
        dealt_output,
        rms,
        grad_input,
        summed[0],
        summed[1],
        grad_qkv_weight,
        summed[2],
        summed[3],
        summed[4],
        grad_out_weight,
        summed[5],
        summed[6],
        summed[7],
        grad_up_weight,
        summed[8],
        grad_down_weight,
        summed[9],
    )


def solution(mesh):
    in_specs = (
        P(("fsdp", "context"), None),
        P(),
        P(),
        P(("fsdp", "context"), None, "tensor"),
        P(None, "tensor"),
        P("tensor", None, None),
        P("tensor", None, None),
        P("tensor", ("fsdp", "context")),
        P(),
        P(),
        P(),
        P(("fsdp", "context"), "tensor"),
        P("tensor"),
        P("tensor", ("fsdp", "context")),
        P(),
        P(),
        P(("fsdp", "context")),
        P(("fsdp", "context"), None),
    )
    out_specs = (
        P(("fsdp", "context"), "tensor", None),
        P(),
        P(("fsdp", "context"), None),
        P(),
        P(),
        P(("fsdp", "context"), None, "tensor"),
        P(None, "tensor"),
        P("tensor", None, None),
        P("tensor", None, None),
        P("tensor", ("fsdp", "context")),
        P(),
        P(),
        P(),
        P(("fsdp", "context"), "tensor"),
        P("tensor"),
        P("tensor", ("fsdp", "context")),
        P(),
    )
    return jax.shard_map(body, mesh=mesh, in_specs=in_specs, out_specs=out_specs, check_vma=False)
```

profile of v0, /device:TPU:0, one launch (start us, length us, event | category | flops | bytes accessed | tf_op | source)
XLA Modules:
  0.0 1227.2 jit_solution(8723379923862665840)
XLA Ops:
  13.2 47.0 %all-gather.13.cloned.1.call-done = f32[768,3,384]{2,0,1:T(8,128)} async-done(((f32[48,3,384]{2,0,1:T(8,128)}), f32[768,3,384]{2,0,1:T(8,128)}) %all-gather.13.cloned.1.call-update) | async-done | bytes 3538960 | tf_op jit(solution)/shard_map/all_gather | solution.py:154
  82.2 43.4 %all-reduce = f32[16]{0:T(128)} all-reduce(f32[16]{0:T(128)S(1)} %dynamic-update-slice), channel_id=1, replica_groups=mesh['fsdp'=4,'context'=4,'tensor'=2] {'fsdp','context'}, use_global_device_ids=true, to_apply=%add | all-reduce | flops 16 | bytes 128
  130.5 31.8 %all-gather.4 = f32[16,6,128]{2,1,0:T(8,128)} all-gather(f32[1,6,128]{2,1,0:T(8,128)S(1)} %bitcast.196), channel_id=3, replica_groups=mesh['fsdp'=4,'context'=4,'tensor'=2] {'fsdp','context'}, dimensions={0}, use_global_device_ids=true | all-gather | bytes 52224 | tf_op jit(solution)/shard_map/all_gather | solution.py:13
  174.0 111.7 %while.22 = (s32[]{:T(128)}, f32[6,128,64]{2,1,0:T(8,128)}, f32[6,128]{1,0:T(8,128)}, s32[]{:T(128)}, f32[16,6,128,64]{2,3,1,0:T(8,128)}, /*index=5*/f32[16]{0:T...) while((s32[]{:T(128)}, f32[6,128,64]{2,1,0:T(8,128)}, f32[6,128]{1,0:T(8,128)}, ...), condition=%wide.region_15.16_spmd.clone, body=%wide.region_14.15_spmd.clone.sunk | while | flops 199685 | bytes 1385643 | solution.py:24
  310.1 33.8 %all-to-all-done.1 = f32[8,64,768]{2,1,0:T(8,128)S(1)} async-done(((f32[8,64,768]{2,1,0:T(8,128)}), f32[8,64,768]{2,1,0:T(8,128)S(1)}, u32[]{:S(2)}, u32[]{:S(2)}) %all-to-all-start.1) | async-done | bytes 1572896 | tf_op jit(solution)/shard_map/all_to_all | solution.py:203
  349.3 11.4 fusion.168
  362.8 47.3 %all-gather.17.cloned.1.call-done = f32[768,1536]{1,0:T(8,128)} async-done(((f32[48,1536]{1,0:T(8,128)}), f32[768,1536]{1,0:T(8,128)}) %all-gather.17.cloned.1.call-update) | async-done | bytes 4718608 | tf_op jit(solution)/shard_map/all_gather | solution.py:156
  410.1 14.9 %fusion.155 = (f32[1536]{0:T(1024)}, f32[512,1536]{1,0:T(8,128)S(1)}, f32[512,1536]{1,0:T(8,128)}) fusion(f32[512,1536]{1,0:T(8,128)} %fusion.168, f32[1536]{0:T(1024)S(1)} %copy-done.118, f32[768,1536]{1,0:T(8,128)} %all-gather.17.cloned.1.call-done, f32[512,768]{1,0:T(8,128)S(1)} %get-tuple-element.631, f32[768]{0:T(1024)S(1)} %copy-done.83, ...), kind=kOutput, calls=%fused_computation.257 | convolution fusion | flops 7265843712 | bytes 15751168 | tf_op jit(solution)/shard_map/dot_general | solution.py:52
  426.6 9.0 fusion.169
  435.9 50.0 %all-reduce.11.cloned.1.call-done = f32[512,768]{1,0:T(8,128)} async-done(((f32[512,768]{1,0:T(8,128)}), f32[512,768]{1,0:T(8,128)}) %all-reduce.11.cloned.1.call-update) | async-done | bytes 1572880 | tf_op jit(solution)/shard_map/psum | solution.py:214
  503.5 12.7 %fusion.38 = f32[512,768]{1,0:T(8,128)} fusion(f32[1536,768]{0,1:T(8,128)} %all-gather.19.cloned.1.call-done, f32[512,1536]{1,0:T(8,128)S(1)} %copy-done.124), kind=kOutput, calls=%fused_computation.80 | convolution fusion | flops 7254048768 | bytes 9437184 | tf_op jit(solution)/shard_map/dot_general | solution.py:53
  517.7 35.5 %all-gather.5 = f32[16,6,128]{2,1,0:T(8,128)} all-gather(f32[1,6,128]{2,1,0:T(8,128)S(1)} %fusion.126), channel_id=5, replica_groups=mesh['fsdp'=4,'context'=4,'tensor'=2] {'fsdp','context'}, dimensions={0}, use_global_device_ids=true | all-gather | bytes 52224 | tf_op jit(solution)/shard_map/all_gather | solution.py:13
  553.3 111.7 %while.23 = (s32[]{:T(128)}, f32[6,128,64]{2,1,0:T(8,128)}, f32[6,128]{1,0:T(8,128)}, s32[]{:T(128)}, f32[16,6,128,64]{2,3,1,0:T(8,128)}, /*index=5*/f32[16]{0:T...) while((s32[]{:T(128)}, f32[6,128,64]{2,1,0:T(8,128)}, ...), condition=%wide.region_31.33_spmd.clone, body=%wide.region_30.32_spmd.clone.sunk | while | flops 199689 | bytes 1385705 | solution.py:24
  688.9 8.5 fusion.13
  727.5 10.4 convolution_bitcast_fusion
  743.5 12.1 fusion.62
  755.6 12.1 fusion.37
  772.7 10.1 fusion.30
  783.6 37.0 %all-reduce.15.cloned.1.call-done = (f32[512,768]{1,0:T(8,128)}, f32[512,768]{1,0:T(8,128)}) async-done(((f32[512,768]{1,0:T(8,128)}, f32[512,768]{1,0:T(8,128)}), (f32[512,768]{1,0:T(8,128)}, f32[512,768]{1,0:T(8,128)})) %all-reduce.15.cloned.1.call-update) | async-done | bytes 3145744 | tf_op jit(solution)/shard_map/psum | solution.py:195
  837.8 89.3 %all-reduce.1 = (f32[3]{0:T(128)S(1)}, f32[768]{0:T(1024)}, f32[768]{0:T(1024)}, f32[3,384]{1,0:T(4,128)}, f32[768]{0:T(1024)}, /*index=5*/f32[768]{0:T(1024)}, f32[768]{0:T(1024)}, f32[1536]{0:T(1024)}, f32[768]{0:T(1024)}) all-reduce(f32[3]{0:T(128)S(1)} %pad_maximum_fusion.5, ...), channel_id=1, replica_groups=mesh['fsdp'=4,'context'=4,'tensor'=2] {'fsdp','context'}, use_global_device_ids=true, to_apply=%region_25.27 | all-reduce | flops 7299 | bytes 58392 | tf_op jit(solution)/shard_map/psum | solution.py:258
  932.4 38.8 %reduce-scatter.9.cloned.1.call-done = f32[48,1536]{1,0:T(8,128)} async-done(((f32[768,1536]{1,0:T(8,128)}), f32[48,1536]{1,0:T(8,128)}) %reduce-scatter.9.cloned.1.call-update) | async-done | bytes 294928 | tf_op jit(solution)/shard_map/reduce_scatter | solution.py:255
  971.2 79.1 %reduce-scatter.11.cloned.1.call-done = f32[1536,48]{0,1:T(8,128)} async-done(((f32[1536,768]{0,1:T(8,128)}), f32[1536,48]{0,1:T(8,128)}) %reduce-scatter.11.cloned.1.call-update) | async-done | bytes 294928 | tf_op jit(solution)/shard_map/reduce_scatter | solution.py:256
  1050.3 95.4 %all-reduce.13.cloned.1.call-done = (f32[6,64,64]{2,1,0:T(8,128)}, f32[6,64,64]{2,1,0:T(8,128)}) async-done(((f32[6,64,64]{2,1,0:T(8,128)}, f32[6,64,64]{2,1,0:T(8,128)}), (f32[6,64,64]{2,1,0:T(8,128)}, f32[6,64,64]{2,1,0:T(8,128)})) %all-reduce.13.cloned.1.call-update) | async-done | bytes 196624 | tf_op jit(solution)/shard_map/psum | solution.py:258
  1145.7 71.5 %reduce-scatter.5.cloned.1.call-done = f32[48,3,384]{2,0,1:T(8,128)} async-done(((f32[768,3,384]{2,0,1:T(8,128)}), f32[48,3,384]{2,0,1:T(8,128)}) %reduce-scatter.5.cloned.1.call-update) | async-done | bytes 221200 | tf_op jit(solution)/shard_map/reduce_scatter | solution.py:253
  (568 shorter events, 387.0 us)
Async XLA Ops:
  7.2 53.1 %all-gather.13.cloned.1.call-start = ((), (), s32[]{:S(2)}) async-start(), calls=%async_computation.6 | async-start | bytes 3760128 | tf_op jit(solution)/shard_map/all_gather | solution.py:154
  8.0 166.0 %all-gather.21.cloned.1.call-start = ((), (), s32[]{:S(2)}) async-start(), calls=%async_computation.16 | async-start | bytes 3342336 | tf_op jit(solution)/shard_map/all_gather | solution.py:13
  13.2 150.8 %copy-start.75 = (f32[512]{0:T(512)}, f32[512]{0:T(512)S(1)}, u32[]{:S(2)}) copy-start(f32[512]{0:T(512)S(1)} %get-tuple-element.642) | copy-start | bytes 6148
  72.0 429.7 %copy-start.58 = (f32[512,6]{0,1:T(8,128)}, f32[512,6]{0,1:T(8,128)S(1)}, u32[]{:S(2)}) copy-start(f32[512,6]{0,1:T(8,128)S(1)} %get-tuple-element.645) | copy-start | bytes 36868
  76.8 220.4 %all-gather.15.cloned.1.call-start = ((), (), s32[]{:S(2)}) async-start(), calls=%async_computation.7 | async-start | bytes 1253376 | tf_op jit(solution)/shard_map/all_gather | solution.py:155
  77.6 271.8 %all-gather.19.cloned.1.call-start = ((), (), s32[]{:S(2)}) async-start(), calls=%async_computation.10 | async-start | bytes 5013504 | tf_op jit(solution)/shard_map/all_gather | solution.py:157
  78.1 282.6 %all-reduce.9.cloned.1.call-start = ((), (), s32[]{:S(2)}) async-start(), calls=%async_computation.8 | async-start | bytes 3145728 | tf_op jit(solution)/shard_map/psum | solution.py:181
  162.6 126.7 %copy-start.2 = (f32[512,6,64]{0,2,1:T(8,128)}, f32[512,6,64]{0,2,1:T(8,128)S(1)}, u32[]{:S(2)}) copy-start(f32[512,6,64]{0,2,1:T(8,128)S(1)} %get-tuple-element.658) | copy-start | bytes 2359300
  162.6 126.7 %copy-start.5 = (f32[512,6,64]{0,2,1:T(8,128)}, f32[512,6,64]{0,2,1:T(8,128)S(1)}, u32[]{:S(2)}) copy-start(f32[512,6,64]{0,2,1:T(8,128)S(1)} %get-tuple-element.659) | copy-start | bytes 2359300
  303.8 106.3 %all-gather.17.cloned.1.call-start = ((), (), s32[]{:S(2)}) async-start(), calls=%async_computation.9 | async-start | bytes 5013504 | tf_op jit(solution)/shard_map/all_gather | solution.py:156
  304.4 39.4 %all-to-all-start.1 = ((f32[8,64,768]{2,1,0:T(8,128)}), f32[8,64,768]{2,1,0:T(8,128)S(1)}, u32[]{:S(2)}, u32[]{:S(2)}) async-start(f32[8,64,768]{2,1,0:T(8,128)} %bitcast.190), calls=%async_computation.1 | async-start | bytes 3145728 | tf_op jit(solution)/shard_map/all_to_all | solution.py:203
  308.0 177.9 %all-reduce.11.cloned.1.call-start = ((), (), s32[]{:S(2)}) async-start(), calls=%async_computation.11 | async-start | bytes 3145728 | tf_op jit(solution)/shard_map/psum | solution.py:214
  309.3 180.0 %copy-start.97 = (f32[512]{0:T(512)}, f32[512]{0:T(512)S(1)}, u32[]{:S(2)}) copy-start(f32[512]{0:T(512)S(1)} %fusion.132) | copy-start | bytes 6148
  362.5 126.2 %copy-start.81 = (f32[512]{0:T(512)}, f32[512]{0:T(512)S(1)}, u32[]{:S(2)}) copy-start(f32[512]{0:T(512)S(1)} %broadcast_multiply_fusion.1) | copy-start | bytes 6148
  362.8 125.9 %copy-start.90 = (f32[512]{0:T(512)}, f32[512]{0:T(512)S(1)}, u32[]{:S(2)}) copy-start(f32[512]{0:T(512)S(1)} %fusion.134) | copy-start | bytes 6148
  435.7 117.6 %all-gather.23.cloned.1.call-start = ((), (), s32[]{:S(2)}) async-start(), calls=%async_computation.17 | async-start | bytes 3342336 | tf_op jit(solution)/shard_map/all_gather | solution.py:13
  497.9 322.7 %all-reduce.15.cloned.1.call-start = ((), (), s32[]{:S(2)}) async-start(), calls=%async_computation.19 | async-start | bytes 6291456 | tf_op jit(solution)/shard_map/psum | solution.py:195
  737.9 194.5 %reduce-scatter.7.cloned.1.call-start = ((), (), s32[]{:S(2)}) async-start(), calls=%async_computation.13 | async-start | bytes 1253376 | tf_op jit(solution)/shard_map/reduce_scatter | solution.py:254
  743.4 227.8 %reduce-scatter.9.cloned.1.call-start = ((), (), s32[]{:S(2)}) async-start(), calls=%async_computation.14 | async-start | bytes 5013504 | tf_op jit(solution)/shard_map/reduce_scatter | solution.py:255
  755.6 294.7 %reduce-scatter.11.cloned.1.call-start = ((), (), s32[]{:S(2)}) async-start(), calls=%async_computation.15 | async-start | bytes 5013504 | tf_op jit(solution)/shard_map/reduce_scatter | solution.py:256
  767.8 377.9 %all-reduce.13.cloned.1.call-start = ((), (), s32[]{:S(2)}) async-start(), calls=%async_computation.18 | async-start | bytes 786432 | tf_op jit(solution)/shard_map/psum | solution.py:258
  772.4 444.8 %reduce-scatter.5.cloned.1.call-start = ((), (), s32[]{:S(2)}) async-start(), calls=%async_computation.12 | async-start | bytes 3760128 | tf_op jit(solution)/shard_map/reduce_scatter | solution.py:253
  828.1 102.2 %all-to-all-start = ((f32[8,64,768]{2,1,0:T(8,128)}), f32[8,64,768]{2,1,0:T(8,128)}, u32[]{:S(2)}, u32[]{:S(2)}) async-start(f32[8,64,768]{2,1,0:T(8,128)} %broadcast_select_fusion.1), calls=%async_computation | async-start | bytes 3145728 | tf_op jit(solution)/shard_map/all_to_all | solution.py:198
  837.0 90.5 %copy-start.49 = (f32[512,768]{1,0:T(8,128)S(1)}, f32[512,768]{1,0:T(8,128)}, u32[]{:S(2)}) copy-start(f32[512,768]{1,0:T(8,128)} %get-tuple-element.616) | copy-start | bytes 4718596
  (117 other events, 1409.7 us)
Sparse Core Ops, SparseCore 0:
  10.4 49.8 all-gather.12
  76.9 44.2 all-gather.20
  123.5 36.9 all-gather.14
  162.7 51.7 all-gather.18
  304.0 50.9 all-reduce.8
  357.1 52.9 all-gather.16
  435.8 50.0 all-reduce.10
  498.0 45.7 all-gather.22
  738.0 82.5 all-reduce.14
  824.7 67.4 reduce-scatter.6
  896.6 74.5 reduce-scatter.8
  975.5 74.7 reduce-scatter.10
  1054.9 90.7 all-reduce.12
  1150.0 67.1 reduce-scatter.4
where the time goes:
time: 1240 us; the launch traced here: 1230 us
  waiting for transfers between devices  503 us (41%)
  blocking collectives  200 us (16%)
  matrix products  192 us (15%)
  other arithmetic  149 us (12%)
  local copies, waits for them, and re-layouts  136 us (11%)
  loops' own time  21.4 us (2%)
  between operations  17.7 us (1%)
    select_n x64, other arithmetic, lap(): return jax.tree.map(lambda a, b: jnp.where(reached, a, b), new, before)  103 us
    dynamic_slice x96, local copies, waits for them, and re-layouts, lap(): new = combine(before, jax.tree.map(lambda part: part[at], everything))  99.5 us
    psum x1, waiting for transfers between devices, body(): lax.psum((grad_ln1_gain, grad_ln1_shift, grad_qkv_bias, grad_feat_query,...  95.4 us
    psum x1, blocking collectives, body(): lax.psum((grad_ln1_gain, grad_ln1_shift, grad_qkv_bias, grad_feat_query,...  89.3 us
    reduce_scatter x1, waiting for transfers between devices, body(): lax.psum_scatter(grad_down_full, ('fsdp', 'context'), scatter_dimension=1...  79.1 us
    reduce_scatter x1, waiting for transfers between devices, body(): lax.psum_scatter(grad_qkv_full, ('fsdp', 'context'), scatter_dimension=0,...  71.5 us
    all_gather x2, blocking collectives, entering(): everything = jax.tree.map(lambda part: lax.all_gather(part, axis), x)  67.3 us
    psum x1, waiting for transfers between devices, body(): grad_normed2 = lax.psum(grad_normed2_part, 'tensor')  50 us
  transfers between devices with their start and end apart: 16, of which 9 were waited for; matrix products, arithmetic and copies ran while one was open for 20% of the time, Pallas kernels for 0%

commit v1 on v0

--- a/solution.py
+++ b/solution.py
@@ -192,7 +192,7 @@
         jnp.where(slot_of[None, :] == counting[:, None], counting[None, :], 0), axis=1
     )
     mlp_terms = mlp_part(normed2, up_full, up_bias, down_full)
-    mlp = lax.psum(mlp_terms, "tensor") + down_bias
+    mlp = jnp.sum(lax.all_gather(mlp_terms, "tensor"), axis=0) + down_bias
     result = hidden + mlp
     outbound = jnp.take(result.reshape(slots, group_rows, width), source_of, axis=0)
     dealt_whole = lax.all_to_all(outbound, "context", split_axis=0, concat_axis=0, tiled=True)

time: 1240 us -> 1240 us (level)
  blocking collectives: 200 us -> 159 us
  waiting for transfers between devices: 503 us -> 531 us
    all_gather x0 -> x1, waiting for transfers between devices: none -> 43.9 us  [body(): mlp = jnp.sum(lax.all_gather(mlp_terms, 'tensor'), axis=0) + down_bias]
    all_to_all x1, waiting for transfers between devices: 0.01 us -> 39.9 us  [body(): lax.all_to_all(outbound, 'context', split_axis=0, concat_axis=0, tiled=True)]
    psum x1, waiting for transfers between devices: 37 us -> 0.02 us  [body(): grad_normed1 = lax.psum(grad_normed1_part, 'tensor')]
    psum x1, blocking collectives: 89.3 us -> 59.3 us  [body(): lax.psum((grad_ln1_gain, grad_ln1_shift, grad_qkv_bias, grad_feat_query,...]
  transfers between devices with their start and end apart: 16 -> 17, of which waited for: 9 -> 11; matrix products, arithmetic and copies ran while one was open for 20% -> 20% of each run, Pallas kernels for 0% -> 0%
where the time goes in v1:
time: 1240 us; the launch traced here: 1220 us
  waiting for transfers between devices  531 us (43%)
  matrix products  192 us (15%)
  blocking collectives  159 us (13%)
  other arithmetic  154 us (12%)
  local copies, waits for them, and re-layouts  138 us (11%)
  loops' own time  21.5 us (2%)
  between operations  18 us (1%)
    select_n x64, other arithmetic, lap(): return jax.tree.map(lambda a, b: jnp.where(reached, a, b), new, before)  103 us
    dynamic_slice x96, local copies, waits for them, and re-layouts, lap(): new = combine(before, jax.tree.map(lambda part: part[at], everything))  100 us
    psum x1, waiting for transfers between devices, body(): lax.psum((grad_ln1_gain, grad_ln1_shift, grad_qkv_bias, grad_feat_query,...  95.3 us
    reduce_scatter x1, waiting for transfers between devices, body(): lax.psum_scatter(grad_down_full, ('fsdp', 'context'), scatter_dimension=1...  79.3 us
    reduce_scatter x1, waiting for transfers between devices, body(): lax.psum_scatter(grad_qkv_full, ('fsdp', 'context'), scatter_dimension=0,...  71.5 us
    all_gather x2, blocking collectives, entering(): everything = jax.tree.map(lambda part: lax.all_gather(part, axis), x)  67.4 us
    psum x1, blocking collectives, body(): lax.psum((grad_ln1_gain, grad_ln1_shift, grad_qkv_bias, grad_feat_query,...  59.3 us
    all_gather x1, waiting for transfers between devices, body(): lax.all_gather(up_weight, ('fsdp', 'context'), axis=0, tiled=True)  47.2 us
  transfers between devices with their start and end apart: 17, of which 11 were waited for; matrix products, arithmetic and copies ran while one was open for 20% of the time, Pallas kernels for 0%

profile of v1, /device:TPU:0, one launch (start us, length us, event | category | flops | bytes accessed | tf_op | source)
XLA Modules:
  0.0 1222.8 jit_solution(16137818308040176953)
XLA Ops:
  13.3 47.0 %all-gather.15.cloned.1.call-done = f32[768,3,384]{2,0,1:T(8,128)} async-done(((f32[48,3,384]{2,0,1:T(8,128)}), f32[768,3,384]{2,0,1:T(8,128)}) %all-gather.15.cloned.1.call-update) | async-done | bytes 3538960 | tf_op jit(solution)/shard_map/all_gather | solution.py:154
  82.3 32.8 %all-reduce = f32[16]{0:T(128)} all-reduce(f32[16]{0:T(128)S(1)} %dynamic-update-slice), channel_id=1, replica_groups=mesh['fsdp'=4,'context'=4,'tensor'=2] {'fsdp','context'}, use_global_device_ids=true, to_apply=%add | all-reduce | flops 16 | bytes 128
  119.9 32.1 %all-gather.5 = f32[16,6,128]{2,1,0:T(8,128)} all-gather(f32[1,6,128]{2,1,0:T(8,128)S(1)} %bitcast.198), channel_id=3, replica_groups=mesh['fsdp'=4,'context'=4,'tensor'=2] {'fsdp','context'}, dimensions={0}, use_global_device_ids=true | all-gather | bytes 52224 | tf_op jit(solution)/shard_map/all_gather | solution.py:13
  163.7 112.8 %while.22 = (s32[]{:T(128)}, f32[6,128,64]{2,1,0:T(8,128)}, f32[6,128]{1,0:T(8,128)}, s32[]{:T(128)}, f32[16,6,128,64]{2,3,1,0:T(8,128)}, /*index=5*/f32[16]{0:T...) while((s32[]{:T(128)}, f32[6,128,64]{2,1,0:T(8,128)}, f32[6,128]{1,0:T(8,128)}, ...), condition=%wide.region_15.16_spmd.clone, body=%wide.region_14.15_spmd.clone.sunk | while | flops 199685 | bytes 1385643 | solution.py:24
  300.9 33.7 %all-to-all-done.1 = f32[8,64,768]{2,1,0:T(8,128)S(1)} async-done(((f32[8,64,768]{2,1,0:T(8,128)}), f32[8,64,768]{2,1,0:T(8,128)S(1)}, u32[]{:S(2)}, u32[]{:S(2)}) %all-to-all-start.1) | async-done | bytes 1572896 | tf_op jit(solution)/shard_map/all_to_all | solution.py:203
  340.1 11.4 fusion.168
  353.6 47.2 %all-gather.19.cloned.1.call-done = f32[768,1536]{1,0:T(8,128)} async-done(((f32[48,1536]{1,0:T(8,128)}), f32[768,1536]{1,0:T(8,128)}) %all-gather.19.cloned.1.call-update) | async-done | bytes 4718608 | tf_op jit(solution)/shard_map/all_gather | solution.py:156
  400.8 14.7 %fusion.155 = (f32[1536]{0:T(1024)}, f32[512,1536]{1,0:T(8,128)S(1)}, f32[512,1536]{1,0:T(8,128)}) fusion(f32[512,1536]{1,0:T(8,128)} %fusion.168, f32[1536]{0:T(1024)S(1)} %copy-done.113, f32[768,1536]{1,0:T(8,128)} %all-gather.19.cloned.1.call-done, f32[512,768]{1,0:T(8,128)S(1)} %get-tuple-element.629, f32[768]{0:T(1024)S(1)} %copy-done.81, ...), kind=kOutput, calls=%fused_computation.257 | convolution fusion | flops 7265843712 | bytes 15751168 | tf_op jit(solution)/shard_map/dot_general | solution.py:52
  417.1 9.0 fusion.169
  426.2 12.4 %fusion.38 = f32[512,768]{1,0:T(8,128)} fusion(f32[1536,768]{0,1:T(8,128)} %all-gather.21.cloned.1.call-done, f32[512,1536]{1,0:T(8,128)} %get-tuple-element.657), kind=kOutput, calls=%fused_computation.80 | convolution fusion | flops 7254048768 | bytes 9437184 | tf_op jit(solution)/shard_map/dot_general | solution.py:53
  438.6 37.8 %all-reduce.10.cloned.1.call-done = f32[512,768]{1,0:T(8,128)} async-done(((f32[512,768]{1,0:T(8,128)}), f32[512,768]{1,0:T(8,128)}) %all-reduce.10.cloned.1.call-update) | async-done | bytes 1572880 | tf_op jit(solution)/shard_map/psum | solution.py:214
  479.0 43.9 %all-gather.25.cloned.1.call-done = f32[1024,768]{1,0:T(8,128)} async-done(((f32[512,768]{1,0:T(8,128)}), f32[1024,768]{1,0:T(8,128)}) %all-gather.25.cloned.1.call-update) | async-done | bytes 3145744 | tf_op jit(solution)/shard_map/all_gather | solution.py:195
  546.0 35.2 %all-gather.6 = f32[16,6,128]{2,1,0:T(8,128)} all-gather(f32[1,6,128]{2,1,0:T(8,128)S(1)} %fusion.126), channel_id=6, replica_groups=mesh['fsdp'=4,'context'=4,'tensor'=2] {'fsdp','context'}, dimensions={0}, use_global_device_ids=true | all-gather | bytes 52224 | tf_op jit(solution)/shard_map/all_gather | solution.py:13
  584.5 112.2 %while.23 = (s32[]{:T(128)}, f32[6,128,64]{2,1,0:T(8,128)}, f32[6,128]{1,0:T(8,128)}, s32[]{:T(128)}, f32[16,6,128,64]{2,3,1,0:T(8,128)}, /*index=5*/f32[16]{0:T...) while((s32[]{:T(128)}, f32[6,128,64]{2,1,0:T(8,128)}, ...), condition=%wide.region_31.33_spmd.clone, body=%wide.region_30.32_spmd.clone.sunk | while | flops 199689 | bytes 1385705 | solution.py:24
  759.6 10.4 convolution_bitcast_fusion
  775.6 11.9 fusion.62
  788.9 11.5 fusion.37
  807.0 9.5 fusion.30
  830.3 39.9 %all-to-all-done = f32[8,64,768]{2,1,0:T(8,128)} async-done(((f32[8,64,768]{2,1,0:T(8,128)}), f32[8,64,768]{2,1,0:T(8,128)}, u32[]{:S(2)}, u32[]{:S(2)}) %all-to-all-start) | async-done | bytes 1572896 | tf_op jit(solution)/shard_map/all_to_all | solution.py:198
  874.8 59.3 %all-reduce.1 = (f32[3]{0:T(128)S(1)}, f32[768]{0:T(1024)}, f32[768]{0:T(1024)}, f32[3,384]{1,0:T(4,128)}, f32[768]{0:T(1024)}, /*index=5*/f32[768]{0:T(1024)}, f32[768]{0:T(1024)}, f32[1536]{0:T(1024)}, f32[768]{0:T(1024)}) all-reduce(f32[3]{0:T(128)S(1)} %pad_maximum_fusion.5, ...), channel_id=1, replica_groups=mesh['fsdp'=4,'context'=4,'tensor'=2] {'fsdp','context'}, use_global_device_ids=true, to_apply=%region_25.27 | all-reduce | flops 7299 | bytes 58392 | tf_op jit(solution)/shard_map/psum | solution.py:258
  937.5 29.1 %reduce-scatter.9.cloned.1.call-done = f32[48,1536]{1,0:T(8,128)} async-done(((f32[768,1536]{1,0:T(8,128)}), f32[48,1536]{1,0:T(8,128)}) %reduce-scatter.9.cloned.1.call-update) | async-done | bytes 294928 | tf_op jit(solution)/shard_map/reduce_scatter | solution.py:255
  966.6 79.3 %reduce-scatter.11.cloned.1.call-done = f32[1536,48]{0,1:T(8,128)} async-done(((f32[1536,768]{0,1:T(8,128)}), f32[1536,48]{0,1:T(8,128)}) %reduce-scatter.11.cloned.1.call-update) | async-done | bytes 294928 | tf_op jit(solution)/shard_map/reduce_scatter | solution.py:256
  1045.9 95.3 %all-reduce.14.cloned.1.call-done = (f32[6,64,64]{2,1,0:T(8,128)}, f32[6,64,64]{2,1,0:T(8,128)}) async-done(((f32[6,64,64]{2,1,0:T(8,128)}, f32[6,64,64]{2,1,0:T(8,128)}), (f32[6,64,64]{2,1,0:T(8,128)}, f32[6,64,64]{2,1,0:T(8,128)})) %all-reduce.14.cloned.1.call-update) | async-done | bytes 196624 | tf_op jit(solution)/shard_map/psum | solution.py:258
  1141.1 71.5 %reduce-scatter.5.cloned.1.call-done = f32[48,3,384]{2,0,1:T(8,128)} async-done(((f32[768,3,384]{2,0,1:T(8,128)}), f32[48,3,384]{2,0,1:T(8,128)}) %reduce-scatter.5.cloned.1.call-update) | async-done | bytes 221200 | tf_op jit(solution)/shard_map/reduce_scatter | solution.py:253
  (559 shorter events, 408.5 us)
Async XLA Ops:
  7.2 53.1 %all-gather.15.cloned.1.call-start = ((), (), s32[]{:S(2)}) async-start(), calls=%async_computation.6 | async-start | bytes 3760128 | tf_op jit(solution)/shard_map/all_gather | solution.py:154
  8.0 155.7 %all-gather.23.cloned.1.call-start = ((), (), s32[]{:S(2)}) async-start(), calls=%async_computation.17 | async-start | bytes 3342336 | tf_op jit(solution)/shard_map/all_gather | solution.py:13
  8.8 70.6 %copy-start.109 = (s32[4,1]{0,1:T(1,128)}, s32[4,1]{0,1:T(1,128)S(1)}, u32[]{:S(2)}) copy-start(s32[4,1]{0,1:T(1,128)S(1)} %reduce-window.4) | copy-start | bytes 52
  13.3 140.5 %copy-start.73 = (f32[512]{0:T(512)}, f32[512]{0:T(512)S(1)}, u32[]{:S(2)}) copy-start(f32[512]{0:T(512)S(1)} %get-tuple-element.644) | copy-start | bytes 6148
  72.0 470.6 %copy-start.56 = (f32[512,6]{0,1:T(8,128)}, f32[512,6]{0,1:T(8,128)S(1)}, u32[]{:S(2)}) copy-start(f32[512,6]{0,1:T(8,128)S(1)} %get-tuple-element.647) | copy-start | bytes 36868
  76.8 211.2 %all-gather.17.cloned.1.call-start = ((), (), s32[]{:S(2)}) async-start(), calls=%async_computation.7 | async-start | bytes 1253376 | tf_op jit(solution)/shard_map/all_gather | solution.py:155
  77.6 262.5 %all-gather.21.cloned.1.call-start = ((), (), s32[]{:S(2)}) async-start(), calls=%async_computation.10 | async-start | bytes 5013504 | tf_op jit(solution)/shard_map/all_gather | solution.py:157
  78.1 273.4 %all-reduce.8.cloned.1.call-start = ((), (), s32[]{:S(2)}) async-start(), calls=%async_computation.8 | async-start | bytes 3145728 | tf_op jit(solution)/shard_map/psum | solution.py:181
  152.3 127.8 %copy-start.2 = (f32[512,6,64]{0,2,1:T(8,128)}, f32[512,6,64]{0,2,1:T(8,128)S(1)}, u32[]{:S(2)}) copy-start(f32[512,6,64]{0,2,1:T(8,128)S(1)} %get-tuple-element.660) | copy-start | bytes 2359300
  152.3 127.8 %copy-start.5 = (f32[512,6,64]{0,2,1:T(8,128)}, f32[512,6,64]{0,2,1:T(8,128)S(1)}, u32[]{:S(2)}) copy-start(f32[512,6,64]{0,2,1:T(8,128)S(1)} %get-tuple-element.661) | copy-start | bytes 2359300
  294.7 106.1 %all-gather.19.cloned.1.call-start = ((), (), s32[]{:S(2)}) async-start(), calls=%async_computation.9 | async-start | bytes 5013504 | tf_op jit(solution)/shard_map/all_gather | solution.py:156
  295.3 39.3 %all-to-all-start.1 = ((f32[8,64,768]{2,1,0:T(8,128)}), f32[8,64,768]{2,1,0:T(8,128)S(1)}, u32[]{:S(2)}, u32[]{:S(2)}) async-start(f32[8,64,768]{2,1,0:T(8,128)} %bitcast.192), calls=%async_computation.1 | async-start | bytes 3145728 | tf_op jit(solution)/shard_map/all_to_all | solution.py:203
  298.9 177.5 %all-reduce.10.cloned.1.call-start = ((), (), s32[]{:S(2)}) async-start(), calls=%async_computation.11 | async-start | bytes 3145728 | tf_op jit(solution)/shard_map/psum | solution.py:214
  353.3 173.0 %copy-start.79 = (f32[512]{0:T(512)}, f32[512]{0:T(512)S(1)}, u32[]{:S(2)}) copy-start(f32[512]{0:T(512)S(1)} %broadcast_multiply_fusion.1) | copy-start | bytes 6148
  353.6 172.7 %copy-start.90 = (f32[512]{0:T(512)}, f32[512]{0:T(512)S(1)}, u32[]{:S(2)}) copy-start(f32[512]{0:T(512)S(1)} %fusion.134) | copy-start | bytes 6148
  426.1 96.7 %all-gather.25.cloned.1.call-start = ((), (), s32[]{:S(2)}) async-start(), calls=%async_computation.18 | async-start | bytes 4718592 | tf_op jit(solution)/shard_map/all_gather | solution.py:195
  438.6 145.9 %all-gather.27.cloned.1.call-start = ((), (), s32[]{:S(2)}) async-start(), calls=%async_computation.19 | async-start | bytes 3342336 | tf_op jit(solution)/shard_map/all_gather | solution.py:13
  538.8 333.8 %all-reduce.12.cloned.1.call-start = ((), (), s32[]{:S(2)}) async-start(), calls=%async_computation.12 | async-start | bytes 3145728 | tf_op jit(solution)/shard_map/psum | solution.py:248
  770.1 167.4 %reduce-scatter.7.cloned.1.call-start = ((), (), s32[]{:S(2)}) async-start(), calls=%async_computation.14 | async-start | bytes 1253376 | tf_op jit(solution)/shard_map/reduce_scatter | solution.py:254
  775.5 191.1 %reduce-scatter.9.cloned.1.call-start = ((), (), s32[]{:S(2)}) async-start(), calls=%async_computation.15 | async-start | bytes 5013504 | tf_op jit(solution)/shard_map/reduce_scatter | solution.py:255
  787.5 258.4 %reduce-scatter.11.cloned.1.call-start = ((), (), s32[]{:S(2)}) async-start(), calls=%async_computation.16 | async-start | bytes 5013504 | tf_op jit(solution)/shard_map/reduce_scatter | solution.py:256
  800.5 340.6 %all-reduce.14.cloned.1.call-start = ((), (), s32[]{:S(2)}) async-start(), calls=%async_computation.20 | async-start | bytes 786432 | tf_op jit(solution)/shard_map/psum | solution.py:258
  806.6 406.0 %reduce-scatter.5.cloned.1.call-start = ((), (), s32[]{:S(2)}) async-start(), calls=%async_computation.13 | async-start | bytes 3760128 | tf_op jit(solution)/shard_map/reduce_scatter | solution.py:253
  823.3 46.9 %all-to-all-start = ((f32[8,64,768]{2,1,0:T(8,128)}), f32[8,64,768]{2,1,0:T(8,128)}, u32[]{:S(2)}, u32[]{:S(2)}) async-start(f32[8,64,768]{2,1,0:T(8,128)} %broadcast_select_fusion.1), calls=%async_computation | async-start | bytes 3145728 | tf_op jit(solution)/shard_map/all_to_all | solution.py:198
  (112 other events, 1232.9 us)
Sparse Core Ops, SparseCore 0:
  10.4 49.8 all-gather.14
  77.0 44.2 all-gather.22
  123.6 36.7 all-gather.16
  162.5 51.8 all-gather.20
  294.8 50.8 all-reduce.7
  347.8 52.9 all-gather.18
  426.3 50.0 all-reduce.9
  477.9 44.8 all-gather.24
  538.9 45.5 all-gather.26
  770.1 50.0 all-reduce.11
  824.4 63.1 reduce-scatter.6
  891.9 74.6 reduce-scatter.8
  971.0 74.7 reduce-scatter.10
  1050.3 90.7 all-reduce.13
  1145.4 67.1 reduce-scatter.4
